TPU v7x, 32 devices: a whole 2x2x4 slice. The times are simulated.
32 devices in a mesh: seq: 8 (over z, y), head: 4 (over x, core).
Axes of the slice: x: 2, y: 2, z: 4, core: 2. Of those that a mesh axis runs over, the one named last changes fastest.
Arguments:
- queries: bfloat16 [4096, 4096], P('seq', 'head'), may hold values from -6 to 6
- keys: bfloat16 [4096, 4096], P('seq', 'head'), may hold values from -6 to 6
- values: bfloat16 [4096, 4096], P('seq', 'head'), may hold values from -6 to 6
- level_weights: float32 [5, 32, 4096], P(None, 'head', 'seq'), may hold values from 0.1 to 3, as said below
- norm_gain: float32 [4096], P('head'), may hold values from 0.25 to 1.75
Outputs:
- mixed: bfloat16 [4096, 4096], P('seq', 'head')
Inputs may be any that keep to these rules, and one draw needn't show every extreme that they name: `level_weights`: positive level weights.
All inputs are finite; a program needn't handle non-finite values.
Results may differ from a plain program's by a relative error of at most 0.0049.
Values may be sent and summed in bfloat16 or wider, within the bound.
No kernel may reach another device: no remote copies, remote signals or barrier semaphores. Data moves between devices by JAX's collectives and lax.ppermute only.
A program may use at most 64 MiB of HBM per device.

v0:
```python
import jax
import jax.numpy as jnp
from jax import lax
from jax.sharding import PartitionSpec as P

HEAD_DIM = 128
STRETCH = 256
D = 4096
EPSILON = 1e-06


def swapped(block, axis, stride):
    count = lax.axis_size(axis)
    route = []
    for low in range(count):
        high = low | 1 << stride
        if high != low and high < count:
            route += [(low, high), (high, low)]
    return lax.ppermute(block, axis, route)


def shifted(block, axis, distance):
    devices = range(lax.axis_size(axis))
    route = [(i - distance, i) for i in devices if i - distance in devices]
    return lax.ppermute(block, axis, route)


def local(queries, keys, values, level_weights, norm_gain):
    tok_rows = queries.shape[0]
    heads_here = queries.shape[1] // HEAD_DIM
    stretch_count = tok_rows // STRETCH
    block_shape = (stretch_count, STRETCH, heads_here, HEAD_DIM)
    query_block_list = queries.reshape(block_shape)
    key_blocks = keys.reshape(block_shape)
    value_blocks = values.reshape(block_shape)
    level_total = level_weights.shape[0]
    weights_here = level_weights.reshape(level_total, heads_here, stretch_count, STRETCH).transpose(
        0, 2, 3, 1
    )
    states = jnp.einsum(
        "cthk,cthv->chkv", key_blocks, value_blocks, preferred_element_type=jnp.float32
    )
    scores = jnp.einsum(
        "cthk,cshk->chts", query_block_list, key_blocks, preferred_element_type=jnp.float32
    )
    causal = lax.broadcasted_iota(jnp.int32, (STRETCH, STRETCH), 0) >= lax.broadcasted_iota(
        jnp.int32, (STRETCH, STRETCH), 1
    )
    attn_probs = jnp.where(causal[None, None], scores, 0.0).astype(jnp.bfloat16)
    intra_out = jnp.einsum(
        "chts,cshv->cthv", attn_probs, value_blocks, preferred_element_type=jnp.float32
    )
    combined = weights_here[0][..., None] * intra_out
    running = states
    local_bits = stretch_count.bit_length() - 1
    level_bit = 0
    groups = running.shape[0] // 2
    block_span = 2**level_bit
    halves = running.reshape(groups, 2, heads_here, HEAD_DIM, HEAD_DIM)
    leftward_sum = halves[:, 0].astype(jnp.bfloat16)
    rightward_queries = query_block_list.reshape(
        groups, 2, block_span * STRETCH, heads_here, HEAD_DIM
    )[:, 1]
    state_readout = jnp.einsum(
        "nthk,nhkv->nthv", rightward_queries, leftward_sum, preferred_element_type=jnp.float32
    )
    level_weight = weights_here[1 + level_bit].reshape(groups, 2, block_span * STRETCH, heads_here)[
        :, 1
    ]
    contrib = level_weight[..., None] * state_readout
    padded = jnp.stack([jnp.zeros_like(contrib), contrib], axis=1)
    combined = combined + padded.reshape(stretch_count, STRETCH, heads_here, HEAD_DIM)
    running = halves[:, 0] + halves[:, 1]
    device_sum = running[0]
    seq_count = lax.axis_size("seq")
    seq_bits = seq_count.bit_length() - 1
    position = lax.axis_index("seq")
    crossing_state_list = []
    for level_bit in range(seq_bits - 1):
        partner = swapped(device_sum, "seq", level_bit)
        is_right = position >> level_bit & 1 == 1
        crossing_state_list.append(
            jnp.where(is_right, partner, jnp.zeros_like(partner)).astype(jnp.bfloat16)
        )
        device_sum = device_sum + partner
    last_partner = shifted(device_sum.astype(jnp.bfloat16), "seq", seq_count // 2)
    crossing_state_list.append(last_partner)
    for number, state_per_level in enumerate(crossing_state_list):
        state_readout = jnp.einsum(
            "lwnx,nxq->lwnq", query_block_list, state_per_level, preferred_element_type=jnp.float32
        )
        combined = combined + weights_here[1 + local_bits + number][..., None] * state_readout
    squares = jnp.sum(combined * combined, axis=(2, 3)).reshape(tok_rows)
    total_squares = lax.psum(squares, "head")
    inverse_rms = lax.rsqrt(total_squares / D + EPSILON)
    flat_out = combined.reshape(tok_rows, heads_here * HEAD_DIM)
    mixed_out = flat_out * inverse_rms[:, None] * norm_gain[None, :]
    return mixed_out.astype(jnp.bfloat16)


def solution(mesh):
    return jax.shard_map(
        local,
        mesh=mesh,
        in_specs=(
            P("seq", "head"),
            P("seq", "head"),
            P("seq", "head"),
            P(None, "head", "seq"),
            P("head"),
        ),
        out_specs=P("seq", "head"),
        check_vma=False,
    )
```

profile of v0, /device:TPU:24, one launch (start us, length us, event | category | flops | bytes accessed | tf_op | source)
XLA Modules:
  0.0 59.7 jit_solution(3533077832521115567)
XLA Ops:
  0.0 1.6 %copy.53 = bf16[64,8,8,128]{3,2,1,0:T(8,128)(2,1)S(1)} copy(bf16[64,8,8,128]{3,1,2,0:T(8,128)(2,1)} %bitcast.103) | data formatting | bytes 2097152
  1.6 0.7 %copy.20 = bf16[2,256,8,128]{1,3,2,0:T(8,128)(2,1)S(1)} copy(bf16[2,256,8,128]{3,2,1,0:T(8,128)(2,1)S(1)} %bitcast.102) | data formatting | bytes 2097152 | tf_op jit(solution)/shard_map/reshape | solution.py:34
  2.3 0.0 copy-start
  2.3 0.0 copy-done.3
  2.3 0.3 copy.54
  2.6 0.0 copy-start.1
  2.6 0.0 copy-start.5
  2.6 0.0 copy-start.4
  2.6 0.4 convolution_bitcast_fusion.1
  3.0 0.2 copy-done
  3.2 0.8 %fusion.17 = f32[8,128,128]{2,1,0:T(8,128)} fusion(f32[1,2,8,128,128]{4,3,2,1,0:T(8,128)S(1)} %convolution_bitcast_fusion.1), kind=kLoop, calls=%fused_computation.27 | loop fusion | flops 131072 | bytes 1572864 | tf_op jit(solution)/shard_map/add | solution.py:73
  4.1 0.0 copy-done.1
  4.1 1.5 %collective-permute-start = (f32[8,128,128]{2,1,0:T(8,128)}, f32[8,128,128]{2,1,0:T(8,128)}, u32[]{:S(2)}, u32[]{:S(2)}) collective-permute-start(f32[8,128,128]{2,1,0:T(8,128)} %fusion.17), channel_id=1, source_target_pairs={{0,4},{4,0},{8,12},{12,8},{16,20},{20,16},{24,28},{28,24},{1,5},{5... | collective-permute-start | bytes 1572872 | tf_op jit(solution)/shard_map/ppermute | solution.py:19
  5.7 0.0 copy-done.5
  5.7 0.0 copy-done.4
  5.7 0.3 copy.52
  6.0 0.3 fusion.7
  6.4 4.2 %fusion.5 = f32[2,8,256,128]{2,3,1,0:T(8,128)} fusion(bf16[2,256,8,128]{1,3,2,0:T(8,128)(2,1)} %copy-done, pred[256,256]{1,0:T(8,128)(4,1)S(1)} %iota_compare_fusion, bf16[2,256,8,128]{3,2,1,0:T(8,128)(2,1)} %bitcast.101, bf16[2,256,8,128]{3,2,1,0:T(8,128)(2,1)S(1)} %bitcast.95), kind=kOutput, calls=%fused_computation.13 | convolution fusion | flops 538968064 | bytes 5308416 | tf_op jit(solution)/shard_map/chts,cshv->cthv/dot_general | solution.py:50
  10.6 7.5 %collective-permute-done = f32[8,128,128]{2,1,0:T(8,128)} collective-permute-done((f32[8,128,128]{2,1,0:T(8,128)}, f32[8,128,128]{2,1,0:T(8,128)}, u32[]{:S(2)}, u32[]{:S(2)}) %collective-permute-start) | collective-permute-done | bytes 524320 | tf_op jit(solution)/shard_map/ppermute | solution.py:19
  18.1 1.1 %fusion.34 = f32[8,128,128]{2,1,0:T(8,128)S(1)} fusion(f32[8,128,128]{2,1,0:T(8,128)} %collective-permute-done, f32[1,2,8,128,128]{4,3,2,1,0:T(8,128)S(1)} %convolution_bitcast_fusion.1), kind=kLoop, calls=%fused_computation.51 | loop fusion | flops 262144 | bytes 2097152 | tf_op jit(solution)/shard_map/add | solution.py:85
  19.2 0.5 collective-permute-start.1
  19.7 0.5 fusion.13
  20.2 11.8 %collective-permute-done.1 = f32[8,128,128]{2,1,0:T(8,128)S(1)} collective-permute-done((f32[8,128,128]{2,1,0:T(8,128)S(1)}, f32[8,128,128]{2,1,0:T(8,128)S(1)}, u32[]{:S(2)}, u32[]{:S(2)}) %collective-permute-start.1) | collective-permute-done | bytes 524320 | tf_op jit(solution)/shard_map/ppermute | solution.py:19
  32.1 0.1 add_convert_fusion
  32.1 0.0 copy-start.2
  32.1 1.4 %collective-permute-start.2 = (bf16[8,128,128]{2,1,0:T(8,128)(2,1)S(1)}, bf16[8,128,128]{2,1,0:T(8,128)(2,1)S(1)}, u32[]{:S(2)}, u32[]{:S(2)}) collective-permute-start(bf16[8,128,128]{2,1,0:T(8,128)(2,1)S(1)} %add_convert_fusion), channel_id=1, source_target_pairs={{0,16},{4,20},{8,24},{12,28},{1,17},{5,21},{9,25},{13,29},{2,18},{... | collective-permute-start | bytes 786440 | tf_op jit(solution)/shard_map/ppermute | solution.py:25
  33.6 0.5 fusion.11
  34.1 12.8 %collective-permute-done.2 = bf16[8,128,128]{2,1,0:T(8,128)(2,1)S(1)} collective-permute-done((bf16[8,128,128]{2,1,0:T(8,128)(2,1)S(1)}, bf16[8,128,128]{2,1,0:T(8,128)(2,1)S(1)}, u32[]{:S(2)}, u32[]{:S(2)}) %collective-permute-start.2) | collective-permute-done | bytes 262176 | tf_op jit(solution)/shard_map/ppermute | solution.py:25
  46.9 2.4 %multiply_reduce_fusion = (f32[2,256]{1,0:T(2,128)S(1)}, f32[2,256,8,128]{1,3,2,0:T(8,128)}) fusion(bf16[2,256,8,128]{3,2,1,0:T(8,128)(2,1)S(1)} %bitcast.98, bf16[8,128,128]{2,1,0:T(8,128)(2,1)S(1)} %collective-permute-done.2, f32[2,256,8]{1,2,0:T(8,128)S(1)} %get-tuple-element.6, f32[8,128,2,256]{3,1,0,2:T(8,128)S(1)} %fusion.11, ...), kind=kOutput, calls=%fused_computation.12 | convolution fusion | flops 139460096 | bytes 10815488 | tf_op jit(solution)/shard_map/lwnx,nxq->lwnq/dot_general | solution.py:89
  49.3 6.8 %psum.7 = f32[512]{0:T(512)S(1)} all-reduce(f32[512]{0:T(512)S(1)} %bitcast.109), channel_id=1, replica_groups=mesh['seq'=8,'head'=4] {'head'}, use_global_device_ids=true, to_apply=%region_1.2 | all-reduce | flops 512 | bytes 4096 | tf_op jit(solution)/shard_map/psum | solution.py:94
  56.1 2.1 %copy.33 = f32[2,256,8,128]{3,2,1,0:T(8,128)S(1)} copy(f32[2,256,8,128]{1,3,2,0:T(8,128)} %get-tuple-element.10) | data formatting | bytes 4194304 | tf_op jit(solution)/shard_map/add | solution.py:92
  58.3 1.4 %fusion.1 = bf16[512,1024]{1,0:T(8,128)(2,1)} fusion(f32[64,8,8,128]{3,2,1,0:T(8,128)S(1)} %bitcast.99, f32[1024]{0:T(1024)S(1)} %copy-done.6, f32[512]{0:T(512)S(1)} %add_rsqrt_fusion), kind=kLoop, calls=%fused_computation.3 | loop fusion | flops 1572864 | bytes 3151872 | tf_op jit(solution)/shard_map/convert_element_type | solution.py:98
  (10 shorter events, 0.1 us)
Async XLA Ops:
  0.0 2.3 %copy-start.3 = (bf16[512,1024]{1,0:T(8,128)(2,1)S(1)}, bf16[512,1024]{1,0:T(8,128)(2,1)}, u32[]{:S(2)}) copy-start(bf16[512,1024]{1,0:T(8,128)(2,1)} %param.7) | copy-start | bytes 3145732
  2.3 1.0 %copy-start = (bf16[2,256,8,128]{1,3,2,0:T(8,128)(2,1)}, bf16[2,256,8,128]{1,3,2,0:T(8,128)(2,1)S(1)}, u32[]{:S(2)}) copy-start(bf16[2,256,8,128]{1,3,2,0:T(8,128)(2,1)S(1)} %copy.20) | copy-start | bytes 3145732
  2.6 1.5 %copy-start.1 = (bf16[64,8,8,128]{3,2,1,0:T(8,128)(2,1)}, bf16[64,8,8,128]{3,2,1,0:T(8,128)(2,1)S(1)}, u32[]{:S(2)}) copy-start(bf16[64,8,8,128]{3,2,1,0:T(8,128)(2,1)S(1)} %copy.54) | copy-start | bytes 3145732
  2.6 3.1 %copy-start.5 = (f32[5,8,512]{2,1,0:T(8,128)S(1)}, f32[5,8,512]{2,1,0:T(8,128)}, u32[]{:S(2)}) copy-start(f32[5,8,512]{2,1,0:T(8,128)} %param.8) | copy-start | bytes 245764
  2.6 3.1 %copy-start.4 = (bf16[512,1024]{1,0:T(8,128)(2,1)S(1)}, bf16[512,1024]{1,0:T(8,128)(2,1)}, u32[]{:S(2)}) copy-start(bf16[512,1024]{1,0:T(8,128)(2,1)} %param.5) | copy-start | bytes 3145732
  4.1 14.0 %collective-permute-start = (f32[8,128,128]{2,1,0:T(8,128)}, f32[8,128,128]{2,1,0:T(8,128)}, u32[]{:S(2)}, u32[]{:S(2)}) collective-permute-start(f32[8,128,128]{2,1,0:T(8,128)} %fusion.17), channel_id=1, source_target_pairs={{0,4},{4,0},{8,12},{12,8},{16,20},{20,16},{24,28},{28,24},{1,5},{5... | collective-permute-start | bytes 1572872 | tf_op jit(solution)/shard_map/ppermute | solution.py:19
  19.2 12.9 %collective-permute-start.1 = (f32[8,128,128]{2,1,0:T(8,128)S(1)}, f32[8,128,128]{2,1,0:T(8,128)S(1)}, u32[]{:S(2)}, u32[]{:S(2)}) collective-permute-start(f32[8,128,128]{2,1,0:T(8,128)S(1)} %fusion.34), channel_id=1, source_target_pairs={{0,8},{8,0},{4,12},{12,4},{16,24},{24,16},{20,28},{28,20},{1,9},{9... | collective-permute-start | bytes 1572872 | tf_op jit(solution)/shard_map/ppermute | solution.py:19
  32.1 14.8 %copy-start.2 = (f32[2,8,256,128]{2,3,1,0:T(8,128)S(1)}, f32[2,8,256,128]{2,3,1,0:T(8,128)}, u32[]{:S(2)}) copy-start(f32[2,8,256,128]{2,3,1,0:T(8,128)} %fusion.5) | copy-start | bytes 6291460
  32.1 14.8 %collective-permute-start.2 = (bf16[8,128,128]{2,1,0:T(8,128)(2,1)S(1)}, bf16[8,128,128]{2,1,0:T(8,128)(2,1)S(1)}, u32[]{:S(2)}, u32[]{:S(2)}) collective-permute-start(bf16[8,128,128]{2,1,0:T(8,128)(2,1)S(1)} %add_convert_fusion), channel_id=1, source_target_pairs={{0,16},{4,20},{8,24},{12,28},{1,17},{5,21},{9,25},{13,29},{2,18},{... | collective-permute-start | bytes 786440 | tf_op jit(solution)/shard_map/ppermute | solution.py:25
  56.1 2.1 %copy-start.6 = (f32[1024]{0:T(1024)S(1)}, f32[1024]{0:T(1024)}, u32[]{:S(2)}) copy-start(f32[1024]{0:T(1024)} %param.9) | copy-start | bytes 12292
where the time goes:
time: 60 us; the launch traced here: 59.7 us
  waiting for transfers between devices  32.2 us (54%)
  matrix products  8.38 us (14%)
  blocking collectives  6.83 us (11%)
  local copies, waits for them, and re-layouts  5.2 us (9%)
  starting transfers between devices  3.46 us (6%)
  other arithmetic  3.45 us (6%)
    ppermute x2, waiting for transfers between devices, swapped(): return lax.ppermute(block, axis, route)  19.3 us
    ppermute x1, waiting for transfers between devices, shifted(): return lax.ppermute(block, axis, route)  12.8 us
    psum x1, blocking collectives, local(): total_squares = lax.psum(squares, 'head')  6.83 us
    dot_general x1, matrix products, local(): jnp.einsum('chts,cshv->cthv', attn_probs, value_blocks, preferred_element...  4.22 us
    dot_general x3, matrix products, local(): jnp.einsum('lwnx,nxq->lwnq', query_block_list, state_per_level, preferred...  3.39 us
    unnamed x18, local copies, waits for them, and re-layouts  2.36 us
    add x1, local copies, waits for them, and re-layouts, local(): combined + weights_here[1 + local_bits + number][..., None] * state_readout  2.12 us
    ppermute x2, starting transfers between devices, swapped(): return lax.ppermute(block, axis, route)  2.03 us
  transfers between devices with their start and end apart: 3, of which 3 were waited for; matrix products, arithmetic and copies ran while one was open for 10% of the time, Pallas kernels for 0%

commit v1 on v0

--- a/solution.py
+++ b/solution.py
@@ -91,7 +91,11 @@
         )
         combined = combined + weights_here[1 + local_bits + number][..., None] * state_readout
     squares = jnp.sum(combined * combined, axis=(2, 3)).reshape(tok_rows)
-    total_squares = lax.psum(squares, "head")
+    total_squares = squares
+    for hop in (1, 2):
+        total_squares = total_squares + lax.ppermute(
+            total_squares, "head", [(dev, dev ^ hop) for dev in range(4)]
+        )
     inverse_rms = lax.rsqrt(total_squares / D + EPSILON)
     flat_out = combined.reshape(tok_rows, heads_here * HEAD_DIM)
     mixed_out = flat_out * inverse_rms[:, None] * norm_gain[None, :]

time: 60 us -> 55.9 us (0.932)
  blocking collectives: 6.83 us -> 0 us
  starting transfers between devices: 3.46 us -> 4.97 us
  waiting for transfers between devices: 32.2 us -> 33.3 us
    psum x1 -> x0, blocking collectives: 6.83 us -> none  [local(): total_squares = lax.psum(squares, 'head')]
    ppermute x0 -> x2, starting transfers between devices: none -> 1.51 us  [local(): lax.ppermute(total_squares, 'head', [(dev, dev ^ hop) for dev in range(4)])]
    ppermute x0 -> x2, waiting for transfers between devices: none -> 1.15 us  [local(): lax.ppermute(total_squares, 'head', [(dev, dev ^ hop) for dev in range(4)])]
  transfers between devices with their start and end apart: 3 -> 5, of which waited for: 3 -> 4; matrix products, arithmetic and copies ran while one was open for 10% -> 14% of each run, Pallas kernels for 0% -> 0%
where the time goes in v1:
time: 55.9 us; the launch traced here: 55.5 us
  waiting for transfers between devices  33.3 us (60%)
  matrix products  8.32 us (15%)
  local copies, waits for them, and re-layouts  5.2 us (9%)
  starting transfers between devices  4.97 us (9%)
  other arithmetic  3.48 us (6%)
    ppermute x2, waiting for transfers between devices, swapped(): return lax.ppermute(block, axis, route)  19.4 us
    ppermute x1, waiting for transfers between devices, shifted(): return lax.ppermute(block, axis, route)  12.8 us
    dot_general x1, matrix products, local(): jnp.einsum('chts,cshv->cthv', attn_probs, value_blocks, preferred_element...  4.19 us
    dot_general x3, matrix products, local(): jnp.einsum('lwnx,nxq->lwnq', query_block_list, state_per_level, preferred...  3.36 us
    unnamed x18, local copies, waits for them, and re-layouts  2.36 us
    add x1, local copies, waits for them, and re-layouts, local(): combined + weights_here[1 + local_bits + number][..., None] * state_readout  2.12 us
    ppermute x2, starting transfers between devices, swapped(): return lax.ppermute(block, axis, route)  2.03 us
    ppermute x2, starting transfers between devices, local(): lax.ppermute(total_squares, 'head', [(dev, dev ^ hop) for dev in range(4)])  1.51 us
  transfers between devices with their start and end apart: 5, of which 4 were waited for; matrix products, arithmetic and copies ran while one was open for 14% of the time, Pallas kernels for 0%

profile of v1, /device:TPU:24, one launch (start us, length us, event | category | flops | bytes accessed | tf_op | source)
XLA Modules:
  0.0 55.5 jit_solution(5017500552953542509)
XLA Ops:
  0.0 1.6 %copy.53 = bf16[64,8,8,128]{3,2,1,0:T(8,128)(2,1)S(1)} copy(bf16[64,8,8,128]{3,1,2,0:T(8,128)(2,1)} %bitcast.103) | data formatting | bytes 2097152
  1.6 0.7 %copy.20 = bf16[2,256,8,128]{1,3,2,0:T(8,128)(2,1)S(1)} copy(bf16[2,256,8,128]{3,2,1,0:T(8,128)(2,1)S(1)} %bitcast.102) | data formatting | bytes 2097152 | tf_op jit(solution)/shard_map/reshape | solution.py:34
  2.3 0.0 copy-start
  2.3 0.3 copy.54
  2.6 0.0 copy-start.5
  2.6 0.0 copy-start.4
  2.6 0.4 convolution_bitcast_fusion.1
  3.0 0.2 copy-done
  3.2 0.9 %fusion.17 = f32[8,128,128]{2,1,0:T(8,128)} fusion(f32[1,2,8,128,128]{4,3,2,1,0:T(8,128)S(1)} %convolution_bitcast_fusion.1), kind=kLoop, calls=%fused_computation.27 | loop fusion | flops 131072 | bytes 1572864 | tf_op jit(solution)/shard_map/add | solution.py:73
  4.1 0.0 copy-done.1
  4.1 1.5 %collective-permute-start = (f32[8,128,128]{2,1,0:T(8,128)}, f32[8,128,128]{2,1,0:T(8,128)}, u32[]{:S(2)}, u32[]{:S(2)}) collective-permute-start(f32[8,128,128]{2,1,0:T(8,128)} %fusion.17), channel_id=1, source_target_pairs={{0,4},{4,0},{8,12},{12,8},{16,20},{20,16},{24,28},{28,24},{1,5},{5... | collective-permute-start | bytes 1572872 | tf_op jit(solution)/shard_map/ppermute | solution.py:19
  5.7 0.0 copy-done.5
  5.7 0.3 copy.52
  6.0 0.3 fusion.7
  6.4 4.2 %fusion.5 = f32[2,8,256,128]{2,3,1,0:T(8,128)} fusion(bf16[2,256,8,128]{1,3,2,0:T(8,128)(2,1)} %copy-done, pred[256,256]{1,0:T(8,128)(4,1)S(1)} %iota_compare_fusion, bf16[2,256,8,128]{3,2,1,0:T(8,128)(2,1)} %bitcast.101, bf16[2,256,8,128]{3,2,1,0:T(8,128)(2,1)S(1)} %bitcast.95), kind=kOutput, calls=%fused_computation.13 | convolution fusion | flops 538968064 | bytes 5308416 | tf_op jit(solution)/shard_map/chts,cshv->cthv/dot_general | solution.py:50
  10.6 7.5 %collective-permute-done = f32[8,128,128]{2,1,0:T(8,128)} collective-permute-done((f32[8,128,128]{2,1,0:T(8,128)}, f32[8,128,128]{2,1,0:T(8,128)}, u32[]{:S(2)}, u32[]{:S(2)}) %collective-permute-start) | collective-permute-done | bytes 524320 | tf_op jit(solution)/shard_map/ppermute | solution.py:19
  18.1 1.1 %fusion.34 = f32[8,128,128]{2,1,0:T(8,128)S(1)} fusion(f32[8,128,128]{2,1,0:T(8,128)} %collective-permute-done, f32[1,2,8,128,128]{4,3,2,1,0:T(8,128)S(1)} %convolution_bitcast_fusion.1), kind=kLoop, calls=%fused_computation.51 | loop fusion | flops 262144 | bytes 2097152 | tf_op jit(solution)/shard_map/add | solution.py:85
  19.2 0.5 collective-permute-start.1
  19.7 0.5 fusion.13
  20.3 11.8 %collective-permute-done.1 = f32[8,128,128]{2,1,0:T(8,128)S(1)} collective-permute-done((f32[8,128,128]{2,1,0:T(8,128)S(1)}, f32[8,128,128]{2,1,0:T(8,128)S(1)}, u32[]{:S(2)}, u32[]{:S(2)}) %collective-permute-start.1) | collective-permute-done | bytes 524320 | tf_op jit(solution)/shard_map/ppermute | solution.py:19
  32.1 0.1 add_convert_fusion
  32.2 1.4 %collective-permute-start.2 = (bf16[8,128,128]{2,1,0:T(8,128)(2,1)S(1)}, bf16[8,128,128]{2,1,0:T(8,128)(2,1)S(1)}, u32[]{:S(2)}, u32[]{:S(2)}) collective-permute-start(bf16[8,128,128]{2,1,0:T(8,128)(2,1)S(1)} %add_convert_fusion), channel_id=1, source_target_pairs={{0,16},{4,20},{8,24},{12,28},{1,17},{5,21},{9,25},{13,29},{2,18},{... | collective-permute-start | bytes 786440 | tf_op jit(solution)/shard_map/ppermute | solution.py:25
  33.6 0.5 fusion.11
  34.1 12.8 %collective-permute-done.2 = bf16[8,128,128]{2,1,0:T(8,128)(2,1)S(1)} collective-permute-done((bf16[8,128,128]{2,1,0:T(8,128)(2,1)S(1)}, bf16[8,128,128]{2,1,0:T(8,128)(2,1)S(1)}, u32[]{:S(2)}, u32[]{:S(2)}) %collective-permute-start.2) | collective-permute-done | bytes 262176 | tf_op jit(solution)/shard_map/ppermute | solution.py:25
  46.9 2.4 %multiply_reduce_fusion = (f32[2,256]{1,0:T(2,128)S(1)}, f32[2,256,8,128]{1,3,2,0:T(8,128)}) fusion(bf16[2,256,8,128]{3,2,1,0:T(8,128)(2,1)S(1)} %bitcast.98, bf16[8,128,128]{2,1,0:T(8,128)(2,1)S(1)} %collective-permute-done.2, f32[2,256,8]{1,2,0:T(8,128)S(1)} %get-tuple-element.6, f32[8,128,2,256]{3,1,0,2:T(8,128)S(1)} %fusion.11, ...), kind=kOutput, calls=%fused_computation.12 | convolution fusion | flops 139460096 | bytes 10815488 | tf_op jit(solution)/shard_map/lwnx,nxq->lwnq/dot_general | solution.py:89
  49.3 0.0 collective-permute-start.3
  49.3 1.1 %collective-permute-done.3 = f32[512]{0:T(512)S(1)} collective-permute-done((f32[512]{0:T(512)S(1)}, f32[512]{0:T(512)S(1)}, u32[]{:S(2)}, u32[]{:S(2)}) %collective-permute-start.3) | collective-permute-done | bytes 2080 | tf_op jit(solution)/shard_map/ppermute | solution.py:96
  50.5 1.5 %collective-permute-start.4 = (f32[512]{0:T(512)S(1)}, f32[512]{0:T(512)S(1)}, u32[]{:S(2)}, u32[]{:S(2)}) collective-permute-start(f32[512]{0:T(512)S(1)} %add.49), channel_id=1, source_target_pairs={{0,2},{1,3},{2,0},{3,1},{4,6},{5,7},{6,4},{7,5},{8,10},{9,11},{10,... | collective-permute-start | bytes 6152 | tf_op jit(solution)/shard_map/ppermute | solution.py:96
  52.0 2.1 %copy.33 = f32[2,256,8,128]{3,2,1,0:T(8,128)S(1)} copy(f32[2,256,8,128]{1,3,2,0:T(8,128)} %get-tuple-element.10) | data formatting | bytes 4194304 | tf_op jit(solution)/shard_map/add | solution.py:92
  54.1 0.0 collective-permute-done.4
  54.1 0.0 copy-done.6
  54.1 1.4 %fusion.1 = bf16[512,1024]{1,0:T(8,128)(2,1)} fusion(f32[64,8,8,128]{3,2,1,0:T(8,128)S(1)} %bitcast.99, f32[1024]{0:T(1024)S(1)} %copy-done.6, f32[512]{0:T(512)S(1)} %add_rsqrt_fusion), kind=kLoop, calls=%fused_computation.3 | loop fusion | flops 1572864 | bytes 3151872 | tf_op jit(solution)/shard_map/convert_element_type | solution.py:102
  (14 shorter events, 0.1 us)
Async XLA Ops:
  0.0 2.3 %copy-start.3 = (bf16[512,1024]{1,0:T(8,128)(2,1)S(1)}, bf16[512,1024]{1,0:T(8,128)(2,1)}, u32[]{:S(2)}) copy-start(bf16[512,1024]{1,0:T(8,128)(2,1)} %param.7) | copy-start | bytes 3145732
  2.3 1.0 %copy-start = (bf16[2,256,8,128]{1,3,2,0:T(8,128)(2,1)}, bf16[2,256,8,128]{1,3,2,0:T(8,128)(2,1)S(1)}, u32[]{:S(2)}) copy-start(bf16[2,256,8,128]{1,3,2,0:T(8,128)(2,1)S(1)} %copy.20) | copy-start | bytes 3145732
  2.6 1.6 %copy-start.1 = (bf16[64,8,8,128]{3,2,1,0:T(8,128)(2,1)}, bf16[64,8,8,128]{3,2,1,0:T(8,128)(2,1)S(1)}, u32[]{:S(2)}) copy-start(bf16[64,8,8,128]{3,2,1,0:T(8,128)(2,1)S(1)} %copy.54) | copy-start | bytes 3145732
  2.6 3.1 %copy-start.5 = (f32[5,8,512]{2,1,0:T(8,128)S(1)}, f32[5,8,512]{2,1,0:T(8,128)}, u32[]{:S(2)}) copy-start(f32[5,8,512]{2,1,0:T(8,128)} %param.8) | copy-start | bytes 245764
  2.6 3.1 %copy-start.4 = (bf16[512,1024]{1,0:T(8,128)(2,1)S(1)}, bf16[512,1024]{1,0:T(8,128)(2,1)}, u32[]{:S(2)}) copy-start(bf16[512,1024]{1,0:T(8,128)(2,1)} %param.5) | copy-start | bytes 3145732
  4.1 14.0 %collective-permute-start = (f32[8,128,128]{2,1,0:T(8,128)}, f32[8,128,128]{2,1,0:T(8,128)}, u32[]{:S(2)}, u32[]{:S(2)}) collective-permute-start(f32[8,128,128]{2,1,0:T(8,128)} %fusion.17), channel_id=1, source_target_pairs={{0,4},{4,0},{8,12},{12,8},{16,20},{20,16},{24,28},{28,24},{1,5},{5... | collective-permute-start | bytes 1572872 | tf_op jit(solution)/shard_map/ppermute | solution.py:19
  19.2 12.9 %collective-permute-start.1 = (f32[8,128,128]{2,1,0:T(8,128)S(1)}, f32[8,128,128]{2,1,0:T(8,128)S(1)}, u32[]{:S(2)}, u32[]{:S(2)}) collective-permute-start(f32[8,128,128]{2,1,0:T(8,128)S(1)} %fusion.34), channel_id=1, source_target_pairs={{0,8},{8,0},{4,12},{12,4},{16,24},{24,16},{20,28},{28,20},{1,9},{9... | collective-permute-start | bytes 1572872 | tf_op jit(solution)/shard_map/ppermute | solution.py:19
  32.2 14.8 %copy-start.2 = (f32[2,8,256,128]{2,3,1,0:T(8,128)S(1)}, f32[2,8,256,128]{2,3,1,0:T(8,128)}, u32[]{:S(2)}) copy-start(f32[2,8,256,128]{2,3,1,0:T(8,128)} %fusion.5) | copy-start | bytes 6291460
  32.2 14.8 %collective-permute-start.2 = (bf16[8,128,128]{2,1,0:T(8,128)(2,1)S(1)}, bf16[8,128,128]{2,1,0:T(8,128)(2,1)S(1)}, u32[]{:S(2)}, u32[]{:S(2)}) collective-permute-start(bf16[8,128,128]{2,1,0:T(8,128)(2,1)S(1)} %add_convert_fusion), channel_id=1, source_target_pairs={{0,16},{4,20},{8,24},{12,28},{1,17},{5,21},{9,25},{13,29},{2,18},{... | collective-permute-start | bytes 786440 | tf_op jit(solution)/shard_map/ppermute | solution.py:25
  49.3 1.2 %collective-permute-start.3 = (f32[512]{0:T(512)S(1)}, f32[512]{0:T(512)S(1)}, u32[]{:S(2)}, u32[]{:S(2)}) collective-permute-start(f32[512]{0:T(512)S(1)} %bitcast.109), channel_id=1, source_target_pairs={{0,1},{1,0},{2,3},{3,2},{4,5},{5,4},{6,7},{7,6},{8,9},{9,8},{10,11... | collective-permute-start | bytes 6152 | tf_op jit(solution)/shard_map/ppermute | solution.py:96
  50.5 3.6 %collective-permute-start.4 = (f32[512]{0:T(512)S(1)}, f32[512]{0:T(512)S(1)}, u32[]{:S(2)}, u32[]{:S(2)}) collective-permute-start(f32[512]{0:T(512)S(1)} %add.49), channel_id=1, source_target_pairs={{0,2},{1,3},{2,0},{3,1},{4,6},{5,7},{6,4},{7,5},{8,10},{9,11},{10,... | collective-permute-start | bytes 6152 | tf_op jit(solution)/shard_map/ppermute | solution.py:96
  52.0 2.2 %copy-start.6 = (f32[1024]{0:T(1024)S(1)}, f32[1024]{0:T(1024)}, u32[]{:S(2)}) copy-start(f32[1024]{0:T(1024)} %param.9) | copy-start | bytes 12292
